TPU v7x, 32 devices: a whole 2x2x4 slice. The times are simulated.
32 devices in a mesh: dp: 16 (over z, y, x), mp: 2 (over core).
Axes of the slice: x: 2, y: 2, z: 4, core: 2. Of those that a mesh axis runs over, the one named last changes fastest.
Arguments:
- gradients: float32 [16, 4, 32, 8192], P('dp', None, 'mp'), may hold values from -6 to 6
- weights: float32 [4, 32, 8192], P(None, 'mp', 'dp'), may hold values from -40 to 40
- first_moment: float32 [4, 32, 8192], P(None, 'mp', 'dp'), may hold values from -0.6 to 0.6
- second_moment: float32 [4, 32, 8192], P(None, 'mp', 'dp'), may hold values from 0.001 to 0.1
- learn_rate: float32 [4], replicated, may hold values from 0.1 to 0.5
- weight_decay: float32 [4], replicated, may hold values from 0.1 to 1
Outputs:
- new_weights: float32 [4, 32, 8192], P(None, 'mp')
- new_first: float32 [4, 32, 8192], P(None, 'mp', 'dp')
- new_second: float32 [4, 32, 8192], P(None, 'mp', 'dp')
- trust_ratio: float32 [4], replicated
All inputs are finite; a program needn't handle non-finite values.
Results may differ from a plain program's by a relative error of at most 0.000062.
Values sent between devices are 32-bit elements; how exact they have to be, the bound alone decides.
No kernel may reach another device: no remote copies, remote signals or barrier semaphores. Data moves between devices by JAX's collectives and lax.ppermute only.
A program may use at most 64 MiB of HBM per device.

v0:
```python
import jax
import jax.numpy as jnp
from jax import lax
from jax.sharding import PartitionSpec as P

STEP = 10


def shards(gradients, weights, first_moment, second_moment, learn_rate, weight_decay):
    replicas = lax.axis_size("dp")
    summed = lax.psum_scatter(gradients, "dp", scatter_dimension=3, tiled=True)[0] * (
        1.0 / replicas
    )
    new_first = 0.9 * first_moment + 0.1 * summed
    new_second = 0.999 * second_moment + 0.001 * summed * summed
    first_fix = 1.0 - 0.9**STEP
    second_fix = 1.0 - 0.999**STEP
    update = (
        new_first / first_fix / (jnp.sqrt(new_second / second_fix) + 1e-06)
        + weight_decay[:, None, None] * weights
    )
    weight_sq, update_sq = lax.psum(
        (jnp.sum(weights * weights, axis=(1, 2)), jnp.sum(update * update, axis=(1, 2))),
        ("dp", "mp"),
    )
    trust_ratio = jnp.sqrt(weight_sq) / (jnp.sqrt(update_sq) + 1e-06)
    stepped = weights - (learn_rate * trust_ratio)[:, None, None] * update
    new_weights = lax.all_gather(stepped, "dp", axis=2, tiled=True)
    return (new_weights, new_first, new_second, trust_ratio)


def solution(mesh):
    in_specs = (
        P("dp", None, "mp", None),
        P(None, "mp", "dp"),
        P(None, "mp", "dp"),
        P(None, "mp", "dp"),
        P(),
        P(),
    )
    out_specs = (P(None, "mp", None), P(None, "mp", "dp"), P(None, "mp", "dp"), P())
    return jax.shard_map(shards, mesh=mesh, in_specs=in_specs, out_specs=out_specs, check_vma=False)
```

profile of v0, /device:TPU:0, one launch (start us, length us, event | category | flops | bytes accessed | tf_op | source)
XLA Modules:
  0.0 205.5 jit_solution(638651230014546051)
XLA Ops:
  7.2 0.0 copy-start
  7.2 0.0 copy-start.3
  7.2 0.0 copy-start.2
  7.2 0.0 copy-start.1
  7.2 0.0 copy-start.4
  7.2 0.0 reduce-scatter.2.cloned.1.call-start
  7.3 0.7 reduce-scatter.2.cloned.1.call-update
  7.9 0.0 all-gather.2.cloned.1.call-start
  8.0 86.7 %reduce-scatter.2.cloned.1.call-done = f32[1,4,16,512]{3,2,1,0:T(8,128)} async-done(((f32[1,4,16,8192]{3,2,1,0:T(8,128)}), f32[1,4,16,512]{3,2,1,0:T(8,128)}) %reduce-scatter.2.cloned.1.call-update) | async-done | bytes 131088 | tf_op jit(solution)/shard_map/reduce_scatter | solution.py:11
  94.7 0.0 copy-done
  94.7 0.0 copy-done.3
  94.7 0.0 copy-done.2
  94.7 0.0 copy-done.1
  94.7 1.7 multiply_reduce_fusion
  96.4 36.8 %all-reduce = (f32[4]{0:T(128)S(1)}, f32[4]{0:T(128)S(1)}) all-reduce(f32[4]{0:T(128)S(1)} %get-tuple-element.8, f32[4]{0:T(128)S(1)} %get-tuple-element.12), channel_id=1, replica_groups=mesh['dp'=16,'mp'=2] {'dp','mp'}, use_global_device_ids=true, to_apply=%region_4.0 | all-reduce | flops 8 | bytes 64 | tf_op jit(solution)/shard_map/psum | solution.py:22
  133.2 0.0 copy-done.4
  133.2 0.5 fusion
  133.7 0.7 multiply_subtract_fusion
  134.4 0.0 all-gather.2.cloned.1.call-update
  134.5 61.1 %all-gather.2.cloned.1.call-done = f32[4,16,8192]{2,1,0:T(8,128)} async-done(((f32[4,16,512]{2,1,0:T(8,128)}), f32[4,16,8192]{2,1,0:T(8,128)}) %all-gather.2.cloned.1.call-update) | async-done | bytes 2097168 | tf_op jit(solution)/shard_map/all_gather | solution.py:28
  195.6 3.1 %copy.11 = f32[4,16,8192]{2,1,0:T(8,128)} copy(f32[4,16,8192]{2,1,0:T(8,128)} %all-gather.2.cloned.1.call-done) | data formatting | bytes 4194304
Async XLA Ops:
  7.2 87.5 %copy-start = (f32[4,16,512]{2,1,0:T(8,128)S(1)}, f32[4,16,512]{2,1,0:T(8,128)}, u32[]{:S(2)}) copy-start(f32[4,16,512]{2,1,0:T(8,128)} %param.7) | copy-start | bytes 393220
  7.2 87.5 %copy-start.3 = (f32[4]{0:T(128)S(1)}, f32[4]{0:T(128)}, u32[]{:S(2)}) copy-start(f32[4]{0:T(128)} %param.11) | copy-start | bytes 52
  7.2 87.5 %copy-start.2 = (f32[4,16,512]{2,1,0:T(8,128)S(1)}, f32[4,16,512]{2,1,0:T(8,128)}, u32[]{:S(2)}) copy-start(f32[4,16,512]{2,1,0:T(8,128)} %param.9) | copy-start | bytes 393220
  7.2 87.5 %copy-start.1 = (f32[4,16,512]{2,1,0:T(8,128)S(1)}, f32[4,16,512]{2,1,0:T(8,128)}, u32[]{:S(2)}) copy-start(f32[4,16,512]{2,1,0:T(8,128)} %param.8) | copy-start | bytes 393220
  7.2 126.0 %copy-start.4 = (f32[4]{0:T(128)S(1)}, f32[4]{0:T(128)}, u32[]{:S(2)}) copy-start(f32[4]{0:T(128)} %param.10) | copy-start | bytes 52
  7.2 87.4 %reduce-scatter.2.cloned.1.call-start = ((), (), s32[]{:S(2)}) async-start(), calls=%async_computation.1 | async-start | bytes 2228224 | tf_op jit(solution)/shard_map/reduce_scatter | solution.py:11
  7.9 187.6 %all-gather.2.cloned.1.call-start = ((), (), s32[]{:S(2)}) async-start(), calls=%async_computation.2 | async-start | bytes 2228224 | tf_op jit(solution)/shard_map/all_gather | solution.py:28
Sparse Core Ops, SparseCore 0:
  10.3 84.3 reduce-scatter.1
  134.6 60.9 all-gather.1
where the time goes:
time: 206 us; the launch traced here: 205 us
  waiting for transfers between devices  148 us (72%)
  blocking collectives  36.8 us (18%)
  between operations  14.1 us (7%)
  local copies, waits for them, and re-layouts  3.08 us (1%)
  other arithmetic  2.97 us (1%)
    reduce_scatter x1, waiting for transfers between devices, shards(): lax.psum_scatter(gradients, 'dp', scatter_dimension=3, tiled=True)[0]  86.7 us
    all_gather x1, waiting for transfers between devices, shards(): new_weights = lax.all_gather(stepped, 'dp', axis=2, tiled=True)  61.1 us
    psum x1, blocking collectives, shards(): lax.psum((jnp.sum(weights * weights, axis=(1, 2)), jnp.sum(update * updat...  36.8 us
  transfers between devices with their start and end apart: 2, of which 2 were waited for; matrix products, arithmetic and copies ran while one was open for 0% of the time, Pallas kernels for 0%

commit v1 on v0

--- a/solution.py
+++ b/solution.py
@@ -25,7 +25,12 @@
     )
     trust_ratio = jnp.sqrt(weight_sq) / (jnp.sqrt(update_sq) + 1e-06)
     stepped = weights - (learn_rate * trust_ratio)[:, None, None] * update
-    new_weights = lax.all_gather(stepped, "dp", axis=2, tiled=True)
+    ring = [stepped]
+    for hop in range(15):
+        ring.append(lax.ppermute(ring[-1], "dp", [(dev, (dev + 1) % 16) for dev in range(16)]))
+    new_weights = jnp.roll(
+        jnp.concatenate(ring[::-1], axis=2), (lax.axis_index("dp") + 1) * ring[0].shape[2], axis=2
+    )
     return (new_weights, new_first, new_second, trust_ratio)
 
 

time: 206 us -> 277 us (1.34)
  waiting for transfers between devices: 148 us -> 217 us
    ppermute x0 -> x15, waiting for transfers between devices: none -> 130 us  [shards(): lax.ppermute(ring[-1], 'dp', [(dev, (dev + 1) % 16) for dev in range(16)])]
    all_gather x1 -> x0, waiting for transfers between devices: 61.1 us -> none  [shards(): new_weights = lax.all_gather(stepped, 'dp', axis=2, tiled=True)]
  transfers between devices with their start and end apart: 2 -> 16, of which waited for: 2 -> 16; matrix products, arithmetic and copies ran while one was open for 0% -> 0% of each run, Pallas kernels for 0% -> 0%
where the time goes in v1:
time: 277 us
  waiting for transfers between devices  217 us (78%)
  blocking collectives  36.8 us (13%)
  between operations  14.3 us (5%)
  other arithmetic  4.08 us (1%)
    ppermute x15, waiting for transfers between devices, shards(): lax.ppermute(ring[-1], 'dp', [(dev, (dev + 1) % 16) for dev in range(16)])  130 us
    reduce_scatter x1, waiting for transfers between devices, shards(): lax.psum_scatter(gradients, 'dp', scatter_dimension=3, tiled=True)[0]  86.7 us
    psum x1, blocking collectives, shards(): lax.psum((jnp.sum(weights * weights, axis=(1, 2)), jnp.sum(update * updat...  36.8 us
  transfers between devices with their start and end apart: 16, of which 16 were waited for; matrix products, arithmetic and copies ran while one was open for 0% of the time, Pallas kernels for 0%

profile of v1, /device:TPU:0, one launch (start us, length us, event | category | flops | bytes accessed | tf_op | source)
XLA Modules:
  0.0 276.5 jit_solution(16021461847107393293)
XLA Ops:
  7.2 0.0 reduce-scatter.2.cloned.1.call-start
  7.2 0.7 reduce-scatter.2.cloned.1.call-update
  7.9 86.7 %reduce-scatter.2.cloned.1.call-done = f32[1,4,16,512]{3,2,1,0:T(8,128)} async-done(((f32[1,4,16,8192]{3,2,1,0:T(8,128)}), f32[1,4,16,512]{3,2,1,0:T(8,128)}) %reduce-scatter.2.cloned.1.call-update) | async-done | bytes 131088 | tf_op jit(solution)/shard_map/reduce_scatter | solution.py:11
  94.6 1.9 multiply_reduce_fusion
  96.5 36.8 %all-reduce = (f32[4]{0:T(128)S(1)}, f32[4]{0:T(128)S(1)}) all-reduce(f32[4]{0:T(128)S(1)} %get-tuple-element.8, f32[4]{0:T(128)S(1)} %get-tuple-element.12), channel_id=1, replica_groups=mesh['dp'=16,'mp'=2] {'dp','mp'}, use_global_device_ids=true, to_apply=%region_4.0 | all-reduce | flops 8 | bytes 64 | tf_op jit(solution)/shard_map/psum | solution.py:22
  133.3 1.2 fusion
  134.5 1.0 multiply_subtract_fusion
  135.5 2.3 collective-permute-start
  137.8 6.3 %collective-permute-done = f32[4,16,512]{2,1,0:T(8,128)S(1)} collective-permute-done((f32[4,16,512]{2,1,0:T(8,128)S(1)}, f32[4,16,512]{2,1,0:T(8,128)S(1)}, u32[]{:S(2)}, u32[]{:S(2)}) %collective-permute-start) | collective-permute-done | bytes 131104 | tf_op jit(solution)/shard_map/ppermute | solution.py:30
  144.1 0.0 collective-permute-start.1
  144.1 8.6 %collective-permute-done.1 = f32[4,16,512]{2,1,0:T(8,128)S(1)} collective-permute-done((f32[4,16,512]{2,1,0:T(8,128)S(1)}, f32[4,16,512]{2,1,0:T(8,128)S(1)}, u32[]{:S(2)}, u32[]{:S(2)}) %collective-permute-start.1) | collective-permute-done | bytes 131104 | tf_op jit(solution)/shard_map/ppermute | solution.py:30
  152.7 0.0 collective-permute-start.2
  152.7 8.6 %collective-permute-done.2 = f32[4,16,512]{2,1,0:T(8,128)S(1)} collective-permute-done((f32[4,16,512]{2,1,0:T(8,128)S(1)}, f32[4,16,512]{2,1,0:T(8,128)S(1)}, u32[]{:S(2)}, u32[]{:S(2)}) %collective-permute-start.2) | collective-permute-done | bytes 131104 | tf_op jit(solution)/shard_map/ppermute | solution.py:30
  161.2 0.0 collective-permute-start.3
  161.2 8.6 %collective-permute-done.3 = f32[4,16,512]{2,1,0:T(8,128)S(1)} collective-permute-done((f32[4,16,512]{2,1,0:T(8,128)S(1)}, f32[4,16,512]{2,1,0:T(8,128)S(1)}, u32[]{:S(2)}, u32[]{:S(2)}) %collective-permute-start.3) | collective-permute-done | bytes 131104 | tf_op jit(solution)/shard_map/ppermute | solution.py:30
  169.8 0.0 collective-permute-start.4
  169.8 9.1 %collective-permute-done.4 = f32[4,16,512]{2,1,0:T(8,128)S(1)} collective-permute-done((f32[4,16,512]{2,1,0:T(8,128)S(1)}, f32[4,16,512]{2,1,0:T(8,128)S(1)}, u32[]{:S(2)}, u32[]{:S(2)}) %collective-permute-start.4) | collective-permute-done | bytes 131104 | tf_op jit(solution)/shard_map/ppermute | solution.py:30
  178.9 0.0 collective-permute-start.5
  178.9 9.7 %collective-permute-done.5 = f32[4,16,512]{2,1,0:T(8,128)S(1)} collective-permute-done((f32[4,16,512]{2,1,0:T(8,128)S(1)}, f32[4,16,512]{2,1,0:T(8,128)S(1)}, u32[]{:S(2)}, u32[]{:S(2)}) %collective-permute-start.5) | collective-permute-done | bytes 131104 | tf_op jit(solution)/shard_map/ppermute | solution.py:30
  188.6 0.0 collective-permute-start.6
  188.6 8.8 %collective-permute-done.6 = f32[4,16,512]{2,1,0:T(8,128)S(1)} collective-permute-done((f32[4,16,512]{2,1,0:T(8,128)S(1)}, f32[4,16,512]{2,1,0:T(8,128)S(1)}, u32[]{:S(2)}, u32[]{:S(2)}) %collective-permute-start.6) | collective-permute-done | bytes 131104 | tf_op jit(solution)/shard_map/ppermute | solution.py:30
  197.4 0.0 collective-permute-start.7
  197.4 8.6 %collective-permute-done.7 = f32[4,16,512]{2,1,0:T(8,128)S(1)} collective-permute-done((f32[4,16,512]{2,1,0:T(8,128)S(1)}, f32[4,16,512]{2,1,0:T(8,128)S(1)}, u32[]{:S(2)}, u32[]{:S(2)}) %collective-permute-start.7) | collective-permute-done | bytes 131104 | tf_op jit(solution)/shard_map/ppermute | solution.py:30
  206.0 0.0 collective-permute-start.8
  206.0 8.6 %collective-permute-done.8 = f32[4,16,512]{2,1,0:T(8,128)S(1)} collective-permute-done((f32[4,16,512]{2,1,0:T(8,128)S(1)}, f32[4,16,512]{2,1,0:T(8,128)S(1)}, u32[]{:S(2)}, u32[]{:S(2)}) %collective-permute-start.8) | collective-permute-done | bytes 131104 | tf_op jit(solution)/shard_map/ppermute | solution.py:30
  214.5 0.0 collective-permute-start.9
  214.5 8.6 %collective-permute-done.9 = f32[4,16,512]{2,1,0:T(8,128)S(1)} collective-permute-done((f32[4,16,512]{2,1,0:T(8,128)S(1)}, f32[4,16,512]{2,1,0:T(8,128)S(1)}, u32[]{:S(2)}, u32[]{:S(2)}) %collective-permute-start.9) | collective-permute-done | bytes 131104 | tf_op jit(solution)/shard_map/ppermute | solution.py:30
  223.1 0.0 collective-permute-start.10
  223.1 8.6 %collective-permute-done.10 = f32[4,16,512]{2,1,0:T(8,128)S(1)} collective-permute-done((f32[4,16,512]{2,1,0:T(8,128)S(1)}, f32[4,16,512]{2,1,0:T(8,128)S(1)}, u32[]{:S(2)}, u32[]{:S(2)}) %collective-permute-start.10) | collective-permute-done | bytes 131104 | tf_op jit(solution)/shard_map/ppermute | solution.py:30
  231.7 0.0 collective-permute-start.11
  231.7 9.1 %collective-permute-done.11 = f32[4,16,512]{2,1,0:T(8,128)S(1)} collective-permute-done((f32[4,16,512]{2,1,0:T(8,128)S(1)}, f32[4,16,512]{2,1,0:T(8,128)S(1)}, u32[]{:S(2)}, u32[]{:S(2)}) %collective-permute-start.11) | collective-permute-done | bytes 131104 | tf_op jit(solution)/shard_map/ppermute | solution.py:30
  240.8 0.0 collective-permute-start.12
  240.8 9.6 %collective-permute-done.12 = f32[4,16,512]{2,1,0:T(8,128)S(1)} collective-permute-done((f32[4,16,512]{2,1,0:T(8,128)S(1)}, f32[4,16,512]{2,1,0:T(8,128)S(1)}, u32[]{:S(2)}, u32[]{:S(2)}) %collective-permute-start.12) | collective-permute-done | bytes 131104 | tf_op jit(solution)/shard_map/ppermute | solution.py:30
  250.5 0.0 collective-permute-start.13
  250.5 8.6 %collective-permute-done.13 = f32[4,16,512]{2,1,0:T(8,128)S(1)} collective-permute-done((f32[4,16,512]{2,1,0:T(8,128)S(1)}, f32[4,16,512]{2,1,0:T(8,128)S(1)}, u32[]{:S(2)}, u32[]{:S(2)}) %collective-permute-start.13) | collective-permute-done | bytes 131104 | tf_op jit(solution)/shard_map/ppermute | solution.py:30
  259.0 0.0 collective-permute-start.14
  259.0 8.6 %collective-permute-done.14 = f32[4,16,512]{2,1,0:T(8,128)S(1)} collective-permute-done((f32[4,16,512]{2,1,0:T(8,128)S(1)}, f32[4,16,512]{2,1,0:T(8,128)S(1)}, u32[]{:S(2)}, u32[]{:S(2)}) %collective-permute-start.14) | collective-permute-done | bytes 131104 | tf_op jit(solution)/shard_map/ppermute | solution.py:30
  268.2 1.5 constant_dynamic-slice_fusion
  (32 shorter events, 0.4 us)
Async XLA Ops:
  7.2 87.4 %reduce-scatter.2.cloned.1.call-start = ((), (), s32[]{:S(2)}) async-start(), calls=%async_computation.1 | async-start | bytes 2228224 | tf_op jit(solution)/shard_map/reduce_scatter | solution.py:11
  135.5 8.6 %collective-permute-start = (f32[4,16,512]{2,1,0:T(8,128)S(1)}, f32[4,16,512]{2,1,0:T(8,128)S(1)}, u32[]{:S(2)}, u32[]{:S(2)}) collective-permute-start(f32[4,16,512]{2,1,0:T(8,128)S(1)} %multiply_subtract_fusion), channel_id=1, source_target_pairs={{0,2},{2,4},{4,6},{6,8},{8,10},{10,12},{12,14},{14,16},{16,18},{18... | collective-permute-start | bytes 393224 | tf_op jit(solution)/shard_map/ppermute | solution.py:30
  144.1 8.6 %collective-permute-start.1 = (f32[4,16,512]{2,1,0:T(8,128)S(1)}, f32[4,16,512]{2,1,0:T(8,128)S(1)}, u32[]{:S(2)}, u32[]{:S(2)}) collective-permute-start(f32[4,16,512]{2,1,0:T(8,128)S(1)} %collective-permute-done), channel_id=1, source_target_pairs={{0,2},{2,4},{4,6},{6,8},{8,10},{10,12},{12,14},{14,16},{16,18},{18... | collective-permute-start | bytes 393224 | tf_op jit(solution)/shard_map/ppermute | solution.py:30
  152.7 8.6 %collective-permute-start.2 = (f32[4,16,512]{2,1,0:T(8,128)S(1)}, f32[4,16,512]{2,1,0:T(8,128)S(1)}, u32[]{:S(2)}, u32[]{:S(2)}) collective-permute-start(f32[4,16,512]{2,1,0:T(8,128)S(1)} %collective-permute-done.1), channel_id=1, source_target_pairs={{0,2},{2,4},{4,6},{6,8},{8,10},{10,12},{12,14},{14,16},{16,18},{18... | collective-permute-start | bytes 393224 | tf_op jit(solution)/shard_map/ppermute | solution.py:30
  161.2 8.6 %collective-permute-start.3 = (f32[4,16,512]{2,1,0:T(8,128)S(1)}, f32[4,16,512]{2,1,0:T(8,128)S(1)}, u32[]{:S(2)}, u32[]{:S(2)}) collective-permute-start(f32[4,16,512]{2,1,0:T(8,128)S(1)} %collective-permute-done.2), channel_id=1, source_target_pairs={{0,2},{2,4},{4,6},{6,8},{8,10},{10,12},{12,14},{14,16},{16,18},{18... | collective-permute-start | bytes 393224 | tf_op jit(solution)/shard_map/ppermute | solution.py:30
  169.8 9.1 %collective-permute-start.4 = (f32[4,16,512]{2,1,0:T(8,128)S(1)}, f32[4,16,512]{2,1,0:T(8,128)S(1)}, u32[]{:S(2)}, u32[]{:S(2)}) collective-permute-start(f32[4,16,512]{2,1,0:T(8,128)S(1)} %collective-permute-done.3), channel_id=1, source_target_pairs={{0,2},{2,4},{4,6},{6,8},{8,10},{10,12},{12,14},{14,16},{16,18},{18... | collective-permute-start | bytes 393224 | tf_op jit(solution)/shard_map/ppermute | solution.py:30
  178.9 9.7 %collective-permute-start.5 = (f32[4,16,512]{2,1,0:T(8,128)S(1)}, f32[4,16,512]{2,1,0:T(8,128)S(1)}, u32[]{:S(2)}, u32[]{:S(2)}) collective-permute-start(f32[4,16,512]{2,1,0:T(8,128)S(1)} %collective-permute-done.4), channel_id=1, source_target_pairs={{0,2},{2,4},{4,6},{6,8},{8,10},{10,12},{12,14},{14,16},{16,18},{18... | collective-permute-start | bytes 393224 | tf_op jit(solution)/shard_map/ppermute | solution.py:30
  188.6 8.8 %collective-permute-start.6 = (f32[4,16,512]{2,1,0:T(8,128)S(1)}, f32[4,16,512]{2,1,0:T(8,128)S(1)}, u32[]{:S(2)}, u32[]{:S(2)}) collective-permute-start(f32[4,16,512]{2,1,0:T(8,128)S(1)} %collective-permute-done.5), channel_id=1, source_target_pairs={{0,2},{2,4},{4,6},{6,8},{8,10},{10,12},{12,14},{14,16},{16,18},{18... | collective-permute-start | bytes 393224 | tf_op jit(solution)/shard_map/ppermute | solution.py:30
  197.4 8.6 %collective-permute-start.7 = (f32[4,16,512]{2,1,0:T(8,128)S(1)}, f32[4,16,512]{2,1,0:T(8,128)S(1)}, u32[]{:S(2)}, u32[]{:S(2)}) collective-permute-start(f32[4,16,512]{2,1,0:T(8,128)S(1)} %collective-permute-done.6), channel_id=1, source_target_pairs={{0,2},{2,4},{4,6},{6,8},{8,10},{10,12},{12,14},{14,16},{16,18},{18... | collective-permute-start | bytes 393224 | tf_op jit(solution)/shard_map/ppermute | solution.py:30
  206.0 8.6 %collective-permute-start.8 = (f32[4,16,512]{2,1,0:T(8,128)S(1)}, f32[4,16,512]{2,1,0:T(8,128)S(1)}, u32[]{:S(2)}, u32[]{:S(2)}) collective-permute-start(f32[4,16,512]{2,1,0:T(8,128)S(1)} %collective-permute-done.7), channel_id=1, source_target_pairs={{0,2},{2,4},{4,6},{6,8},{8,10},{10,12},{12,14},{14,16},{16,18},{18... | collective-permute-start | bytes 393224 | tf_op jit(solution)/shard_map/ppermute | solution.py:30
  214.5 8.6 %collective-permute-start.9 = (f32[4,16,512]{2,1,0:T(8,128)S(1)}, f32[4,16,512]{2,1,0:T(8,128)S(1)}, u32[]{:S(2)}, u32[]{:S(2)}) collective-permute-start(f32[4,16,512]{2,1,0:T(8,128)S(1)} %collective-permute-done.8), channel_id=1, source_target_pairs={{0,2},{2,4},{4,6},{6,8},{8,10},{10,12},{12,14},{14,16},{16,18},{18... | collective-permute-start | bytes 393224 | tf_op jit(solution)/shard_map/ppermute | solution.py:30
  223.1 8.6 %collective-permute-start.10 = (f32[4,16,512]{2,1,0:T(8,128)S(1)}, f32[4,16,512]{2,1,0:T(8,128)S(1)}, u32[]{:S(2)}, u32[]{:S(2)}) collective-permute-start(f32[4,16,512]{2,1,0:T(8,128)S(1)} %collective-permute-done.9), channel_id=1, source_target_pairs={{0,2},{2,4},{4,6},{6,8},{8,10},{10,12},{12,14},{14,16},{16,18},{18... | collective-permute-start | bytes 393224 | tf_op jit(solution)/shard_map/ppermute | solution.py:30
  231.7 9.1 %collective-permute-start.11 = (f32[4,16,512]{2,1,0:T(8,128)S(1)}, f32[4,16,512]{2,1,0:T(8,128)S(1)}, u32[]{:S(2)}, u32[]{:S(2)}) collective-permute-start(f32[4,16,512]{2,1,0:T(8,128)S(1)} %collective-permute-done.10), channel_id=1, source_target_pairs={{0,2},{2,4},{4,6},{6,8},{8,10},{10,12},{12,14},{14,16},{16,18},{18... | collective-permute-start | bytes 393224 | tf_op jit(solution)/shard_map/ppermute | solution.py:30
  240.8 9.6 %collective-permute-start.12 = (f32[4,16,512]{2,1,0:T(8,128)S(1)}, f32[4,16,512]{2,1,0:T(8,128)S(1)}, u32[]{:S(2)}, u32[]{:S(2)}) collective-permute-start(f32[4,16,512]{2,1,0:T(8,128)S(1)} %collective-permute-done.11), channel_id=1, source_target_pairs={{0,2},{2,4},{4,6},{6,8},{8,10},{10,12},{12,14},{14,16},{16,18},{18... | collective-permute-start | bytes 393224 | tf_op jit(solution)/shard_map/ppermute | solution.py:30
  250.5 8.6 %collective-permute-start.13 = (f32[4,16,512]{2,1,0:T(8,128)S(1)}, f32[4,16,512]{2,1,0:T(8,128)S(1)}, u32[]{:S(2)}, u32[]{:S(2)}) collective-permute-start(f32[4,16,512]{2,1,0:T(8,128)S(1)} %collective-permute-done.12), channel_id=1, source_target_pairs={{0,2},{2,4},{4,6},{6,8},{8,10},{10,12},{12,14},{14,16},{16,18},{18... | collective-permute-start | bytes 393224 | tf_op jit(solution)/shard_map/ppermute | solution.py:30
  259.0 8.6 %collective-permute-start.14 = (f32[4,16,512]{2,1,0:T(8,128)S(1)}, f32[4,16,512]{2,1,0:T(8,128)S(1)}, u32[]{:S(2)}, u32[]{:S(2)}) collective-permute-start(f32[4,16,512]{2,1,0:T(8,128)S(1)} %collective-permute-done.13), channel_id=1, source_target_pairs={{0,2},{2,4},{4,6},{6,8},{8,10},{10,12},{12,14},{14,16},{16,18},{18... | collective-permute-start | bytes 393224 | tf_op jit(solution)/shard_map/ppermute | solution.py:30
Sparse Core Ops, SparseCore 0:
  10.2 84.3 reduce-scatter.1
